TPU v7x, 32 devices: a whole 2x2x4 slice. The times are simulated.
32 devices in a mesh: grp: 2 (over y), tm: 4 (over z), tmpl: 2 (over x), chan: 2 (over core).
Axes of the slice: x: 2, y: 2, z: 4, core: 2. Of those that a mesh axis runs over, the one named last changes fastest.
Arguments:
- record: bfloat16 [32, 4096], P('chan', ('grp', 'tm')), parts along dimension 1, may hold values from -640 to 640
- templates: bfloat16 [2, 768, 32, 512], P('tmpl', 'tm', 'chan'), may hold values from -0.046875 to 0.046875
- span_list: int32 [8, 4], P(('grp', 'tm')), parts along dimension 0, may hold values from -1 to 3, as said below
Outputs:
- scan_out: float32 [1536, 4096], P(('tmpl', 'chan'), ('grp', 'tm')), parts along dimension 1
There are 2 independent parts, one for each index of `grp`. A program takes and returns all parts, laid end to end along the dimension named above; an argument that names none is the same for every part. Nothing has to cross between parts.
Inputs may be any that keep to these rules, and one draw needn't show every extreme that they name: `span_list`: each shard lists distinct blocks in its first slots and -1 in the rest; between 1 and 4 blocks a shard, exactly 8 in all shards together, and some shard lists 4.
All inputs are finite; a program needn't handle non-finite values.
Results may differ from a plain program's by a relative error of at most 0.0003.
Values may be sent and summed in bfloat16 or wider, within the bound.
A program may use at most 64 MiB of HBM per device.

v0:
```python
import jax
import jax.numpy as jnp
from jax import lax
from jax.sharding import PartitionSpec as P

C = 32
L = 512
SPAN = 128
MOST_DENSE = 4


def from_behind(block, axis, distance):
    devices = range(lax.axis_size(axis))
    route = [(i - distance, i) for i in devices if i - distance in devices]
    return lax.ppermute(block, axis, route)


def windows(segment):
    seg_len = segment.shape[1]
    tiled = jnp.tile(segment, (1, SPAN + 1))
    flattened = tiled[:, : SPAN * (seg_len + 1)]
    return flattened.reshape(segment.shape[0], SPAN, seg_len + 1)[:, :, :L]


def slot_windows(extended, own_list):
    stacked = []
    for slot in range(MOST_DENSE):
        span_at = own_list[slot]
        segment = lax.dynamic_slice_in_dim(extended, jnp.maximum(span_at, 0) * SPAN, SPAN + L, 1)
        stacked.append(jnp.where(span_at >= 0, windows(segment), jnp.zeros((), extended.dtype)))
    return jnp.stack(stacked)


def local(record, templates, span_list):
    own_list = span_list[0]
    following = from_behind(record, "tm", -1)
    extended = jnp.concatenate([record, following], axis=1)
    own_windows = slot_windows(extended, own_list)
    product = jnp.einsum(
        "kcl,qcrl->kqr",
        lax.all_gather(templates, "tm", axis=1, tiled=True)[0],
        own_windows,
        preferred_element_type=jnp.float32,
    )
    product = product.reshape(product.shape[0], MOST_DENSE * SPAN)
    summed = lax.psum_scatter(product, "chan", scatter_dimension=0, tiled=True)
    local_energy = jnp.sum(jnp.square(own_windows.astype(jnp.float32)), axis=(1, 3)).reshape(-1)
    energy = lax.psum(local_energy, "chan")
    return summed * lax.rsqrt(energy / (C * L) + 1e-05)[None, :]


def solution(mesh):
    in_specs = (P("chan", ("grp", "tm")), P("tmpl", "tm", "chan", None), P(("grp", "tm"), None))
    out_specs = P(("tmpl", "chan"), ("grp", "tm"))
    return jax.shard_map(local, mesh=mesh, in_specs=in_specs, out_specs=out_specs, check_vma=False)
```

profile of v0, /device:TPU:0, one launch (start us, length us, event | category | flops | bytes accessed | tf_op | source)
XLA Modules:
  0.0 266.6 jit_solution(5071008891932363301)
XLA Ops:
  6.5 5.3 %copy.6 = bf16[1,192,16,512]{3,1,2,0:T(8,128)(2,1)} copy(bf16[1,192,16,512]{3,2,1,0:T(8,128)(2,1)} %param.4) | data formatting | bytes 6291456 | tf_op args[1]
  11.8 0.0 all-gather.2.cloned.1.call-update
  11.8 0.0 reduce-scatter.2.cloned.1.call-start
  11.9 0.6 copy-done.2
  12.5 1.3 collective-permute-start
  13.8 0.7 fusion.7
  19.8 0.2 tile.16
  20.0 0.3 copy.9
  20.4 0.2 slice.52
  20.6 8.1 %reshape.67 = bf16[16,128,641]{2,1,0:T(8,128)(2,1)} reshape(bf16[16,82048]{1,0:T(8,128)(2,1)S(1)} %slice.52) | data formatting | bytes 5251072 | tf_op jit(solution)/shard_map/reshape | solution.py:22
  28.6 0.2 tile.42
  28.9 0.3 copy.12
  29.2 0.2 slice.58
  29.4 7.9 %reshape.70 = bf16[16,128,641]{2,1,0:T(8,128)(2,1)} reshape(bf16[16,82048]{1,0:T(8,128)(2,1)S(1)} %slice.58) | data formatting | bytes 5251072 | tf_op jit(solution)/shard_map/reshape | solution.py:22
  37.3 0.2 tile.40
  37.5 0.3 copy.11
  37.8 0.2 slice.56
  38.0 7.9 %reshape.69 = bf16[16,128,641]{2,1,0:T(8,128)(2,1)} reshape(bf16[16,82048]{1,0:T(8,128)(2,1)S(1)} %slice.56) | data formatting | bytes 5251072 | tf_op jit(solution)/shard_map/reshape | solution.py:22
  45.9 0.2 tile.18
  46.1 0.3 copy.10
  46.4 0.2 slice.54
  46.6 8.1 %reshape.68 = bf16[16,128,641]{2,1,0:T(8,128)(2,1)} reshape(bf16[16,82048]{1,0:T(8,128)(2,1)S(1)} %slice.54) | data formatting | bytes 5251072 | tf_op jit(solution)/shard_map/reshape | solution.py:22
  54.7 4.1 %fusion.2 = (bf16[1,16,128,512]{3,2,1,0:T(8,128)(2,1)S(1)}, bf16[1,16,128,512]{3,2,1,0:T(8,128)(2,1)}) fusion(bf16[16,128,641]{2,1,0:T(8,128)(2,1)} %reshape.70, pred[]{:T(512)} %bitcast.9, bf16[16,128,641]{2,1,0:T(8,128)(2,1)} %reshape.69, pred[]{:T(512)} %bitcast.6), kind=kLoop, calls=%fused_computation.5 | loop fusion | flops 2097152 | bytes 8388610 | tf_op jit(solution)/shard_map/stack | solution.py:31
  58.8 0.8 copy-done.1
  59.7 2.2 fusion.4
  61.9 171.0 %all-gather.2.cloned.1.call-done = bf16[1,768,16,512]{3,1,2,0:T(8,128)(2,1)} async-done(((bf16[1,192,16,512]{3,1,2,0:T(8,128)(2,1)}), bf16[1,768,16,512]{3,1,2,0:T(8,128)(2,1)}) %all-gather.2.cloned.1.call-update) | async-done | bytes 12582928 | tf_op jit(solution)/shard_map/all_gather | solution.py:41
  232.9 14.3 %fusion = f32[4,128,768,1]{2,1,3,0:T(8,128)} fusion(bf16[1,768,16,512]{3,1,2,0:T(8,128)(2,1)} %all-gather.2.cloned.1.call-done, bf16[1,16,128,512]{3,2,1,0:T(8,128)(2,1)S(1)} %get-tuple-element.13, bf16[1,16,128,512]{3,2,1,0:T(8,128)(2,1)} %get-tuple-element.14, bf16[1,16,128,512]{3,2,1,0:T(8,128)(2,1)} %get-tuple-element.15, ...), kind=kOutput, calls=%fused_computation.1 | convolution fusion | flops 6455033856 | bytes 22544384 | tf_op jit(solution)/shard_map/kcl,qcrl->kqr/dot_general | solution.py:39
  247.2 3.0 %copy.7 = f32[768,512]{1,0:T(8,128)} copy(f32[768,512]{0,1:T(8,128)} %bitcast.43) | data formatting | bytes 3145728 | tf_op jit(solution)/shard_map/reshape | solution.py:45
  250.3 4.3 %multiply_reduce_fusion = f32[4,128]{1,0:T(4,128)S(1)} fusion(bf16[1,16,128,512]{3,2,1,0:T(8,128)(2,1)S(1)} %get-tuple-element.13, bf16[1,16,128,512]{3,2,1,0:T(8,128)(2,1)} %get-tuple-element.14, bf16[1,16,128,512]{3,2,1,0:T(8,128)(2,1)} %get-tuple-element.15, bf16[1,16,128,512]{3,2,1,0:T(8,128)(2,1)} %get-tuple-element.16), kind=kLoop, calls=%fused_computation | loop fusion | flops 25165312 | bytes 8390656 | tf_op jit(solution)/shard_map/reduce_sum | solution.py:47
  254.6 2.5 psum.7
  257.1 0.6 reduce-scatter.2.cloned.1.call-done
  257.7 2.1 broadcast_multiply_fusion
  (13 shorter events, 0.1 us)
Async XLA Ops:
  6.5 226.4 %all-gather.2.cloned.1.call-start = ((), (), s32[]{:S(2)}) async-start(), calls=%async_computation.1 | async-start | bytes 15728640 | tf_op jit(solution)/shard_map/all_gather | solution.py:41
  11.8 0.7 copy-start.2
  11.8 2.0 copy-start.3
  11.8 245.8 %reduce-scatter.2.cloned.1.call-start = ((), (), s32[]{:S(2)}) async-start(), calls=%async_computation.2 | async-start | bytes 2359296 | tf_op jit(solution)/shard_map/reduce_scatter | solution.py:46
  12.5 7.2 %collective-permute-start = (bf16[16,512]{1,0:T(8,128)(2,1)S(1)}, bf16[16,512]{1,0:T(8,128)(2,1)S(1)}, u32[]{:S(2)}, u32[]{:S(2)}) collective-permute-start(bf16[16,512]{1,0:T(8,128)(2,1)S(1)} %copy-done.2), channel_id=1, source_target_pairs={{4,0},{8,4},{12,8},{5,1},{9,5},{13,9},{6,2},{10,6},{14,10},{7,3},{... | collective-permute-start | bytes 49160 | tf_op jit(solution)/shard_map/ppermute | solution.py:15
  54.7 4.1 %copy-start = (bf16[16,128,641]{2,1,0:T(8,128)(2,1)S(1)}, bf16[16,128,641]{2,1,0:T(8,128)(2,1)}, u32[]{:S(2)}) copy-start(bf16[16,128,641]{2,1,0:T(8,128)(2,1)} %reshape.67) | copy-start | bytes 7876612
  54.7 4.9 %copy-start.1 = (bf16[16,128,641]{2,1,0:T(8,128)(2,1)S(1)}, bf16[16,128,641]{2,1,0:T(8,128)(2,1)}, u32[]{:S(2)}) copy-start(bf16[16,128,641]{2,1,0:T(8,128)(2,1)} %reshape.68) | copy-start | bytes 7876612
Sparse Core Ops, SparseCore 0:
  12.0 220.8 all-gather.1
  250.4 7.2 reduce-scatter.1
where the time goes:
time: 267 us
  waiting for transfers between devices  172 us (64%)
  local copies, waits for them, and re-layouts  45.3 us (17%)
  between operations  18.8 us (7%)
  matrix products  14.3 us (5%)
  other arithmetic  12.8 us (5%)
    all_gather x1, waiting for transfers between devices, local(): lax.all_gather(templates, 'tm', axis=1, tiled=True)[0]  171 us
    reshape x4, local copies, waits for them, and re-layouts, windows(): return flattened.reshape(segment.shape[0], SPAN, seg_len + 1)[:, :, :L]  31.9 us
    dot_general x1, matrix products, local(): jnp.einsum('kcl,qcrl->kqr', lax.all_gather(templates, 'tm', axis=1, tiled...  14.3 us
    unnamed x14, local copies, waits for them, and re-layouts  8.11 us
    another operation x2, other arithmetic, slot_windows(): return jnp.stack(stacked)  6.34 us
  transfers between devices with their start and end apart: 3, of which 2 were waited for; matrix products, arithmetic and copies ran while one was open for 17% of the time, Pallas kernels for 0%

commit v1 on v0

--- a/solution.py
+++ b/solution.py
@@ -32,13 +32,47 @@
 
 
 def local(record, templates, span_list):
+
+    def _number_chunk(target, d0):
+        left_arr = lax.psum(1, "tm")
+        w1, big, carry_in = (left_arr, lax.axis_index("tm"), target.shape[d0])
+        leaves = []
+        for ix, u in enumerate(target.shape):
+            leaves.append(u * w1 if ix == d0 else u)
+        o_now = jnp.zeros(leaves, target.dtype)
+        local_next = lax.dynamic_update_slice_in_dim(o_now, target, big * carry_in, axis=d0)
+        z_new = opened = target
+        w = 1
+        while w < w1 // 2 + 1:
+            pool = []
+            ix = 0
+            while ix < w1:
+                pool.append((ix, (ix + 1) % w1))
+                ix = ix + 1
+            z_new = lax.ppermute(z_new, "tm", pool)
+            local_next = lax.dynamic_update_slice_in_dim(
+                local_next, z_new, (big - w) % w1 * carry_in, axis=d0
+            )
+            if 2 * w < w1:
+                history = []
+                ix = 0
+                while ix < w1:
+                    history.append((ix, (ix - 1) % w1))
+                    ix += 1
+                opened = lax.ppermute(opened, "tm", history)
+                local_next = lax.dynamic_update_slice_in_dim(
+                    local_next, opened, (big + w) % w1 * carry_in, axis=d0
+                )
+            w = w + 1
+        return local_next
+
     own_list = span_list[0]
     following = from_behind(record, "tm", -1)
     extended = jnp.concatenate([record, following], axis=1)
     own_windows = slot_windows(extended, own_list)
     product = jnp.einsum(
         "kcl,qcrl->kqr",
-        lax.all_gather(templates, "tm", axis=1, tiled=True)[0],
+        _number_chunk(templates, 1)[0],
         own_windows,
         preferred_element_type=jnp.float32,
     )

time: 267 us -> 305 us (1.14)
  local copies, waits for them, and re-layouts: 45.3 us -> 68.1 us
  waiting for transfers between devices: 172 us -> 187 us
  starting transfers between devices: 1.32 us -> 6.34 us
  other arithmetic: 12.8 us -> 9.33 us
    all_gather x1 -> x0, waiting for transfers between devices: 171 us -> none  [local(): lax.all_gather(templates, 'tm', axis=1, tiled=True)[0]]
    ppermute x1, waiting for transfers between devices: 0.01 us -> 115 us  [from_behind(): return lax.ppermute(block, axis, route)]
    ppermute x0 -> x3, waiting for transfers between devices: none -> 69.3 us  [the longest x2 69.3 us: _number_chunk(): z_new = lax.ppermute(z_new, 'tm', pool)]
    dynamic_update_slice x0 -> x4, local copies, waits for them, and re-layouts: none -> 20.9 us  [the longest x2 12.1 us: _number_chunk(): lax.dynamic_update_slice_in_dim(local_next, z_new, (big - w) % w1 * carry...]
    squeeze x0 -> x1, local copies, waits for them, and re-layouts: none -> 5.74 us  [local(): _number_chunk(templates, 1)[0]]
    ppermute x0 -> x3, starting transfers between devices: none -> 5.05 us  [the longest x2 3.03 us: _number_chunk(): z_new = lax.ppermute(z_new, 'tm', pool)]
    unnamed x14 -> x19, local copies, waits for them, and re-layouts: 8.11 us -> 4.28 us
    another operation x2, other arithmetic: 6.34 us -> 2.92 us  [slot_windows(): return jnp.stack(stacked)]
  transfers between devices with their start and end apart: 3 -> 5, of which waited for: 2 -> 3; matrix products, arithmetic and copies ran while one was open for 17% -> 21% of each run, Pallas kernels for 0% -> 0%
where the time goes in v1:
time: 305 us
  waiting for transfers between devices  187 us (61%)
  local copies, waits for them, and re-layouts  68.1 us (22%)
  between operations  18.8 us (6%)
  matrix products  12.4 us (4%)
  other arithmetic  9.33 us (3%)
  starting transfers between devices  6.34 us (2%)
    ppermute x1, waiting for transfers between devices, from_behind(): return lax.ppermute(block, axis, route)  115 us
    ppermute x2, waiting for transfers between devices, _number_chunk(): z_new = lax.ppermute(z_new, 'tm', pool)  69.3 us
    reshape x4, local copies, waits for them, and re-layouts, windows(): return flattened.reshape(segment.shape[0], SPAN, seg_len + 1)[:, :, :L]  31.9 us
    dot_general x1, matrix products, local(): jnp.einsum('kcl,qcrl->kqr', _number_chunk(templates, 1)[0], own_windows,...  12.4 us
    dynamic_update_slice x2, local copies, waits for them, and re-layouts, _number_chunk(): lax.dynamic_update_slice_in_dim(local_next, z_new, (big - w) % w1 * carry...  12.1 us
  transfers between devices with their start and end apart: 5, of which 3 were waited for; matrix products, arithmetic and copies ran while one was open for 21% of the time, Pallas kernels for 0%

profile of v1, /device:TPU:0, one launch (start us, length us, event | category | flops | bytes accessed | tf_op | source)
XLA Modules:
  0.0 304.5 jit_solution(14031956946285210062)
XLA Ops:
  6.5 3.0 collective-permute-start
  9.6 2.0 collective-permute-start.1
  11.6 69.3 %collective-permute-done = bf16[1,192,16,512]{3,2,1,0:T(8,128)(2,1)} collective-permute-done((bf16[1,192,16,512]{3,2,1,0:T(8,128)(2,1)}, bf16[1,192,16,512]{3,2,1,0:T(8,128)(2,1)}, u32[]{:S(2)}, u32[]{:S(2)}) %collective-permute-start) | collective-permute-done | bytes 3145760 | tf_op jit(solution)/shard_map/ppermute | solution.py:52
  80.9 1.3 collective-permute-start.3
  82.2 0.7 constant_dynamic-update-slice_fusion.1
  82.9 5.7 %squeeze.16 = bf16[768,16,512]{2,0,1:T(8,128)(2,1)} broadcast(bf16[]{:T(256)} %constant.52.clone.1), dimensions={} | broadcast | bytes 12582914 | tf_op jit(solution)/shard_map/squeeze | solution.py:75
  88.6 3.4 %copy_dynamic-update-slice_fusion.3 = bf16[768,16,512]{2,0,1:T(8,128)(2,1)} fusion(bf16[768,16,512]{2,0,1:T(8,128)(2,1)} %squeeze.16, s32[]{:T(128)S(6)} %select_n.65, bf16[192,16,512]{2,1,0:T(8,128)(2,1)S(1)} %bitcast.44), kind=kLoop, calls=%fused_computation.7 | loop fusion | bytes 6291460 | tf_op jit(solution)/shard_map/dynamic_update_slice | solution.py:43
  92.0 0.7 fusion.7
  98.0 114.7 %collective-permute-done.3 = bf16[16,512]{1,0:T(8,128)(2,1)S(1)} collective-permute-done((bf16[16,512]{1,0:T(8,128)(2,1)}, bf16[16,512]{1,0:T(8,128)(2,1)S(1)}, u32[]{:S(2)}, u32[]{:S(2)}) %collective-permute-start.3) | collective-permute-done | bytes 16416 | tf_op jit(solution)/shard_map/ppermute | solution.py:15
  212.7 0.2 tile.40
  212.9 0.3 copy.17
  213.5 8.0 %reshape.77 = bf16[16,128,641]{2,1,0:T(8,128)(2,1)} reshape(bf16[16,82048]{1,0:T(8,128)(2,1)S(1)} %slice.56) | data formatting | bytes 5251072 | tf_op jit(solution)/shard_map/reshape | solution.py:22
  221.5 0.2 tile.42
  221.7 0.3 copy.18
  222.2 7.9 %reshape.78 = bf16[16,128,641]{2,1,0:T(8,128)(2,1)} reshape(bf16[16,82048]{1,0:T(8,128)(2,1)S(1)} %slice.58) | data formatting | bytes 5251072 | tf_op jit(solution)/shard_map/reshape | solution.py:22
  230.3 0.3 copy.15
  230.8 7.8 %reshape.75 = bf16[16,128,641]{2,1,0:T(8,128)(2,1)} reshape(bf16[16,82048]{1,0:T(8,128)(2,1)S(1)} %slice.52) | data formatting | bytes 5251072 | tf_op jit(solution)/shard_map/reshape | solution.py:22
  238.9 0.3 copy.16
  239.4 8.1 %reshape.76 = bf16[16,128,641]{2,1,0:T(8,128)(2,1)} reshape(bf16[16,82048]{1,0:T(8,128)(2,1)S(1)} %slice.54) | data formatting | bytes 5251072 | tf_op jit(solution)/shard_map/reshape | solution.py:22
  247.6 2.6 fusion.2
  250.2 0.5 copy-done
  250.7 1.7 copy-done.1
  252.4 0.3 fusion.4
  252.7 6.8 %copy_dynamic-update-slice_fusion.2 = bf16[768,16,512]{2,0,1:T(8,128)(2,1)} fusion(bf16[768,16,512]{2,0,1:T(8,128)(2,1)} %copy_dynamic-update-slice_fusion.3, s32[]{:T(128)S(6)} %select_n.67, bf16[192,16,512]{2,1,0:T(8,128)(2,1)} %bitcast.1), kind=kLoop, calls=%fused_computation.6 | loop fusion | bytes 6291460 | tf_op jit(solution)/shard_map/dynamic_update_slice | solution.py:53
  259.5 5.4 %copy_dynamic-update-slice_fusion.1 = bf16[768,16,512]{2,0,1:T(8,128)(2,1)} fusion(bf16[768,16,512]{2,0,1:T(8,128)(2,1)} %copy_dynamic-update-slice_fusion.2, s32[]{:T(128)S(6)} %select_n.69, bf16[192,16,512]{2,1,0:T(8,128)(2,1)} %bitcast.2), kind=kLoop, calls=%fused_computation.5 | loop fusion | bytes 6291460 | tf_op jit(solution)/shard_map/dynamic_update_slice | solution.py:63
  264.9 5.3 %copy_dynamic-update-slice_fusion = bf16[768,16,512]{2,0,1:T(8,128)(2,1)} fusion(bf16[768,16,512]{2,0,1:T(8,128)(2,1)} %copy_dynamic-update-slice_fusion.1, s32[]{:T(128)S(6)} %select_n.71, bf16[192,16,512]{2,1,0:T(8,128)(2,1)} %bitcast.3), kind=kLoop, calls=%fused_computation.4 | loop fusion | bytes 6291460 | tf_op jit(solution)/shard_map/dynamic_update_slice | solution.py:53
  270.2 12.4 %fusion = f32[768,4,128,1]{0,2,3,1:T(8,128)} fusion(bf16[768,16,512]{2,0,1:T(8,128)(2,1)} %copy_dynamic-update-slice_fusion, bf16[1,16,128,512]{3,2,1,0:T(8,128)(2,1)S(1)} %get-tuple-element.13, bf16[1,16,128,512]{3,2,1,0:T(8,128)(2,1)S(1)} %get-tuple-element.14, bf16[1,16,128,512]{3,2,1,0:T(8,128)(2,1)S(1)} %get-tuple-element.15, ...), kind=kOutput, calls=%fused_computation.1 | convolution fusion | flops 6476005376 | bytes 22544384 | tf_op jit(solution)/shard_map/kcl,qcrl->kqr/dot_general | solution.py:73
  282.7 3.0 copy.13
  285.7 4.3 %multiply_reduce_fusion = f32[4,128]{1,0:T(4,128)S(1)} fusion(bf16[1,16,128,512]{3,2,1,0:T(8,128)(2,1)S(1)} %get-tuple-element.13, bf16[1,16,128,512]{3,2,1,0:T(8,128)(2,1)} %copy-done.2, bf16[1,16,128,512]{3,2,1,0:T(8,128)(2,1)} %copy-done.3, bf16[1,16,128,512]{3,2,1,0:T(8,128)(2,1)} %copy-done.4), kind=kLoop, calls=%fused_computation | loop fusion | flops 25165312 | bytes 8390656 | tf_op jit(solution)/shard_map/reduce_sum | solution.py:81
  290.0 2.5 psum.7
  292.5 3.1 %reduce-scatter.2.cloned.1.call-done = f32[384,512]{1,0:T(8,128)} async-done(((f32[768,512]{1,0:T(8,128)}), f32[384,512]{1,0:T(8,128)}) %reduce-scatter.2.cloned.1.call-update) | async-done | bytes 786448 | tf_op jit(solution)/shard_map/reduce_scatter | solution.py:80
  295.6 2.1 broadcast_multiply_fusion
  (26 shorter events, 1.2 us)
Async XLA Ops:
  6.5 289.0 %reduce-scatter.2.cloned.1.call-start = ((), (), s32[]{:S(2)}) async-start(), calls=%async_computation.1 | async-start | bytes 2359296 | tf_op jit(solution)/shard_map/reduce_scatter | solution.py:80
  6.5 74.3 %collective-permute-start = (bf16[1,192,16,512]{3,2,1,0:T(8,128)(2,1)}, bf16[1,192,16,512]{3,2,1,0:T(8,128)(2,1)}, u32[]{:S(2)}, u32[]{:S(2)}) collective-permute-start(bf16[1,192,16,512]{3,2,1,0:T(8,128)(2,1)} %param.4), channel_id=1, source_target_pairs={{0,4},{4,8},{8,12},{12,0},{1,5},{5,9},{9,13},{13,1},{2,6},{6,10},{... | collective-permute-start | bytes 9437192 | tf_op jit(solution)/shard_map/ppermute | solution.py:52
  9.6 250.0 %collective-permute-start.1 = (bf16[1,192,16,512]{3,2,1,0:T(8,128)(2,1)}, bf16[1,192,16,512]{3,2,1,0:T(8,128)(2,1)}, u32[]{:S(2)}, u32[]{:S(2)}) collective-permute-start(bf16[1,192,16,512]{3,2,1,0:T(8,128)(2,1)} %param.4), channel_id=1, source_target_pairs={{0,12},{4,0},{8,4},{12,8},{1,13},{5,1},{9,5},{13,9},{2,14},{6,2},{... | collective-permute-start | bytes 9437192 | tf_op jit(solution)/shard_map/ppermute | solution.py:62
  80.9 184.0 %collective-permute-start.2 = (bf16[1,192,16,512]{3,2,1,0:T(8,128)(2,1)}, bf16[1,192,16,512]{3,2,1,0:T(8,128)(2,1)}, u32[]{:S(2)}, u32[]{:S(2)}) collective-permute-start(bf16[1,192,16,512]{3,2,1,0:T(8,128)(2,1)} %collective-permute-done), channel_id=1, source_target_pairs={{0,4},{4,8},{8,12},{12,0},{1,5},{5,9},{9,13},{13,1},{2,6},{6,10},{... | collective-permute-start | bytes 9437192 | tf_op jit(solution)/shard_map/ppermute | solution.py:52
  80.9 131.8 %collective-permute-start.3 = (bf16[16,512]{1,0:T(8,128)(2,1)}, bf16[16,512]{1,0:T(8,128)(2,1)S(1)}, u32[]{:S(2)}, u32[]{:S(2)}) collective-permute-start(bf16[16,512]{1,0:T(8,128)(2,1)} %param.3), channel_id=1, source_target_pairs={{4,0},{8,4},{12,8},{5,1},{9,5},{13,9},{6,2},{10,6},{14,10},{7,3},{... | collective-permute-start | bytes 49160 | tf_op jit(solution)/shard_map/ppermute | solution.py:15
  82.9 5.7 %copy-start.5 = (bf16[1,192,16,512]{3,2,1,0:T(8,128)(2,1)S(1)}, bf16[1,192,16,512]{3,2,1,0:T(8,128)(2,1)}, u32[]{:S(2)}) copy-start(bf16[1,192,16,512]{3,2,1,0:T(8,128)(2,1)} %param.4) | copy-start | bytes 9437188
  88.6 3.4 %copy-start.6 = (s32[1,4]{1,0:T(1,128)S(1)}, s32[1,4]{1,0:T(1,128)}, u32[]{:S(2)}) copy-start(s32[1,4]{1,0:T(1,128)} %param.5) | copy-start | bytes 52
  247.6 3.2 %copy-start = (bf16[16,128,641]{2,1,0:T(8,128)(2,1)S(1)}, bf16[16,128,641]{2,1,0:T(8,128)(2,1)}, u32[]{:S(2)}) copy-start(bf16[16,128,641]{2,1,0:T(8,128)(2,1)} %reshape.75) | copy-start | bytes 7876612
  247.6 4.9 %copy-start.1 = (bf16[16,128,641]{2,1,0:T(8,128)(2,1)S(1)}, bf16[16,128,641]{2,1,0:T(8,128)(2,1)}, u32[]{:S(2)}) copy-start(bf16[16,128,641]{2,1,0:T(8,128)(2,1)} %reshape.76) | copy-start | bytes 7876612
  250.2 20.0 %copy-start.2 = (bf16[1,16,128,512]{3,2,1,0:T(8,128)(2,1)}, bf16[1,16,128,512]{3,2,1,0:T(8,128)(2,1)S(1)}, u32[]{:S(2)}) copy-start(bf16[1,16,128,512]{3,2,1,0:T(8,128)(2,1)S(1)} %get-tuple-element.14) | copy-start | bytes 6291460
  252.7 17.5 %copy-start.3 = (bf16[1,16,128,512]{3,2,1,0:T(8,128)(2,1)}, bf16[1,16,128,512]{3,2,1,0:T(8,128)(2,1)S(1)}, u32[]{:S(2)}) copy-start(bf16[1,16,128,512]{3,2,1,0:T(8,128)(2,1)S(1)} %get-tuple-element.15) | copy-start | bytes 6291460
  252.7 17.5 %copy-start.4 = (bf16[1,16,128,512]{3,2,1,0:T(8,128)(2,1)}, bf16[1,16,128,512]{3,2,1,0:T(8,128)(2,1)S(1)}, u32[]{:S(2)}) copy-start(bf16[1,16,128,512]{3,2,1,0:T(8,128)(2,1)S(1)} %get-tuple-element.16) | copy-start | bytes 6291460
Sparse Core Ops, SparseCore 0:
  285.8 9.6 reduce-scatter.1
